TPU v7x, 32 devices: a whole 2x2x4 slice. The times are simulated.
32 devices in a mesh: seq: 8 (over y, x, core), weight: 4 (over z).
Axes of the slice: x: 2, y: 2, z: 4, core: 2. Of those that a mesh axis runs over, the one named last changes fastest.
Arguments:
- tokens: bfloat16 [4, 4096, 1024], P('weight', 'seq'), may hold values from -6 to 6
- cotangent: bfloat16 [4, 4096, 1024], P('weight', 'seq'), may hold values from -6 to 6
- offsets: int32 [4, 3], P('weight'), may hold values from 0 to 4096, as said below
- qkv_weight: bfloat16 [2, 1024, 3072], P(None, 'weight'), may hold values from -0.1875 to 0.1875
- attn_out_weight: bfloat16 [2, 1024, 1024], P(None, 'weight'), may hold values from -0.75 to 0.75
- mlp_in_weight: bfloat16 [2, 1024, 5248], P(None, 'weight'), may hold values from -0.1875 to 0.1875
- mlp_out_weight: bfloat16 [2, 2624, 1024], P(None, None, 'weight'), may hold values from -0.125 to 0.125
- norm_gains: bfloat16 [2, 2, 1024], P(None, None, 'weight'), may hold values from 0.5 to 1.5
Outputs:
- output: bfloat16 [4, 4096, 1024], P('weight', 'seq')
- input_grad: float32 [4, 4096, 1024], P('weight', 'seq')
- grad_qkv: float32 [2, 1024, 3072], P(None, 'weight')
- grad_attn_out: float32 [2, 1024, 1024], P(None, 'weight')
- grad_mlp_in: float32 [2, 1024, 5248], P(None, 'weight')
- grad_mlp_out: float32 [2, 2624, 1024], P(None, None, 'weight')
- grad_gains: float32 [2, 2, 1024], P(None, None, 'weight')
Inputs may be any that keep to these rules, and one draw needn't show every extreme that they name: offsets[g] = (0, c, 4096): a group holds two sequences, tokens 0 to c - 1 and c to 4095, with c from 1024 to 3072.
All inputs are finite; a program needn't handle non-finite values.
Results may differ from a plain program's by a relative error of at most 0.025.
Values may be sent and summed in bfloat16 or wider, within the bound.
No kernel may reach another device: no remote copies, remote signals or barrier semaphores. Data moves between devices by JAX's collectives and lax.ppermute only.
A program may use at most 384 MiB of HBM per device.

v0:
```python
import jax
import jax.numpy as jnp
from jax import lax
from jax.sharding import PartitionSpec as P

HEADS = 16
HEAD_DIM = 64
HALF = 64


EPS = 1e-05
THETA = 10000.0
NEG = -1e30


def padded(cells, sides, width):
    for axis, dim in sides:
        count = lax.axis_size(axis)
        ends = count - 1
        head = lax.slice_in_dim(cells, 0, width, axis=dim)
        tail = lax.slice_in_dim(cells, cells.shape[dim] - width, cells.shape[dim], axis=dim)
        cells = jnp.concatenate(
            [
                lax.ppermute(tail, axis, [(i, (i + 1) % count) for i in range(ends)]),
                cells,
                lax.ppermute(head, axis, [((i + 1) % count, i) for i in range(ends)]),
            ],
            axis=dim,
        )
    return cells


def layer_norm(values, gain):
    center = values - jnp.mean(values, axis=-1, keepdims=True)
    spread = jnp.mean(center * center, axis=-1, keepdims=True)
    return center * lax.rsqrt(spread + EPS) * gain


def seq_start(places, bounds):
    return jnp.where(places >= bounds[1], bounds[1], 0)


def rotate(values, places):
    half = HEAD_DIM // 2
    freq = THETA ** (-2.0 * jnp.arange(half, dtype=jnp.float32) / HEAD_DIM)
    angle = places.astype(jnp.float32)[:, None] * freq[None, :]
    cosine = jnp.concatenate([jnp.cos(angle), jnp.cos(angle)], axis=1)[:, None, :]
    sine = jnp.concatenate([jnp.sin(angle), jnp.sin(angle)], axis=1)[:, None, :]
    heads = values.reshape(values.shape[0], HEADS, HEAD_DIM)
    turned = jnp.concatenate([-heads[..., half:], heads[..., :half]], axis=-1)
    return (heads * cosine + turned * sine).reshape(values.shape)


def window_mask(query_glob, key_glob, bounds, total_rows):
    near = jnp.abs(query_glob[:, None] - key_glob[None, :]) <= HALF
    inside = (key_glob >= 0) & (key_glob < total_rows)
    same = seq_start(query_glob, bounds)[:, None] == seq_start(key_glob, bounds)[None, :]
    return near & inside[None, :] & same


def geglu(gate_up):
    width = gate_up.shape[1] // 2
    return jax.nn.gelu(gate_up[:, :width], approximate=False) * gate_up[:, width:]


def inner(left, right):
    return lax.dot_general(
        left, right, (((0,), (0,)), ((), ())), preferred_element_type=jnp.float32
    )


def outer(left, right):
    return lax.dot_general(
        left, right, (((1,), (1,)), ((), ())), preferred_element_type=jnp.float32
    )


def split_heads(values):
    return values.reshape(values.shape[0], HEADS, HEAD_DIM)


def attn_scores(queries, key_wide, window):
    raw = jnp.einsum(
        "qhd,khd->hqk",
        split_heads(queries),
        split_heads(key_wide),
        preferred_element_type=jnp.float32,
    )
    return jnp.where(window[None], raw * HEAD_DIM ** (-0.5), NEG)


def fetch_forward(pieces):
    return (
        lax.all_gather(pieces[0], "weight", axis=0, tiled=True),
        lax.all_gather(pieces[1], "weight", axis=0, tiled=True),
        lax.all_gather(pieces[2], "weight", axis=0, tiled=True),
        lax.all_gather(pieces[3], "weight", axis=1, tiled=True),
        lax.all_gather(pieces[4], "weight", axis=1, tiled=True),
    )


def fetch_backward(pieces):
    return (
        lax.all_gather(pieces[0], "weight", axis=0, tiled=True),
        lax.all_gather(pieces[1], "weight", axis=0, tiled=True),
        lax.all_gather(pieces[2], "weight", axis=0, tiled=True),
        lax.all_gather(pieces[3], "weight", axis=1, tiled=True),
        lax.all_gather(pieces[4], "weight", axis=1, tiled=True),
    )


def layer_forward(stream, weights, places, window):
    w_qkv, w_attn, w_in, w_out, gain_low = weights
    gain = gain_low.astype(jnp.float32)
    width = stream.shape[1]
    normed = layer_norm(stream, gain[0]).astype(jnp.bfloat16)
    mixed = jnp.dot(normed, w_qkv, preferred_element_type=jnp.float32)
    queries = rotate(mixed[:, :width], places).astype(jnp.bfloat16)
    keys = rotate(mixed[:, width : 2 * width], places).astype(jnp.bfloat16)
    values = mixed[:, 2 * width :].astype(jnp.bfloat16)
    kv_wide = padded(jnp.concatenate([keys, values], axis=1), (("seq", 0),), HALF)
    scores = attn_scores(queries, kv_wide[:, :width], window)
    top = jnp.max(scores, axis=-1, keepdims=True)
    log_total = top + jnp.log(jnp.sum(jnp.exp(scores - top), axis=-1, keepdims=True))
    prob = jnp.exp(scores - log_total).astype(jnp.bfloat16)
    context = jnp.einsum(
        "hqk,khd->qhd", prob, split_heads(kv_wide[:, width:]), preferred_element_type=jnp.float32
    )
    context = context.reshape(stream.shape).astype(jnp.bfloat16)
    middle = stream + jnp.dot(context, w_attn, preferred_element_type=jnp.float32)
    shaped = layer_norm(middle, gain[1]).astype(jnp.bfloat16)
    gate_up = jnp.dot(shaped, w_in, preferred_element_type=jnp.float32)
    hidden = geglu(gate_up).astype(jnp.bfloat16)
    result = middle + jnp.dot(hidden, w_out, preferred_element_type=jnp.float32)
    return (
        result,
        (stream, normed, queries, kv_wide, log_total, context, middle, shaped, gate_up, hidden),
    )


def layer_backward(upstream, weights, saved_acts, places, window):
    w_qkv, w_attn, w_in, w_out, gain_low = weights
    gain = gain_low.astype(jnp.float32)
    stream, normed, queries, kv_wide, log_total, context, middle, shaped, gate_up, hidden = (
        saved_acts
    )
    width = stream.shape[1]
    rows_here = stream.shape[0]
    up_low = upstream.astype(jnp.bfloat16)
    grad_out = inner(hidden, up_low)
    d_hidden = outer(up_low, w_out)
    d_gate_up = jax.vjp(geglu, gate_up)[1](d_hidden)[0].astype(jnp.bfloat16)
    grad_in = inner(shaped, d_gate_up)
    d_shaped = outer(d_gate_up, w_in)
    mid_part, gain_two = jax.vjp(layer_norm, middle, gain[1])[1](d_shaped)
    d_middle = upstream + mid_part
    mid_low = d_middle.astype(jnp.bfloat16)
    grad_attn = inner(context, mid_low)
    d_context = outer(mid_low, w_attn).astype(jnp.bfloat16)
    key_wide = kv_wide[:, :width]
    value_wide = kv_wide[:, width:]
    prob = jnp.exp(attn_scores(queries, key_wide, window) - log_total)
    context_heads = split_heads(d_context)
    d_prob = jnp.einsum(
        "qhd,khd->hqk", context_heads, split_heads(value_wide), preferred_element_type=jnp.float32
    )
    delta = jnp.sum(prob * d_prob, axis=-1, keepdims=True)
    d_score = (prob * (d_prob - delta)).astype(jnp.bfloat16)
    scale = HEAD_DIM ** (-0.5)
    d_query = (
        jnp.einsum(
            "hqk,khd->qhd", d_score, split_heads(key_wide), preferred_element_type=jnp.float32
        )
        * scale
    )
    d_key = (
        jnp.einsum(
            "hqk,qhd->khd", d_score, split_heads(queries), preferred_element_type=jnp.float32
        )
        * scale
    )
    d_value = jnp.einsum(
        "hqk,qhd->khd", prob.astype(jnp.bfloat16), context_heads, preferred_element_type=jnp.float32
    )
    d_kv = jnp.concatenate(
        [d_key.reshape(key_wide.shape), d_value.reshape(value_wide.shape)], axis=1
    )
    rims = jnp.concatenate([d_kv[:HALF], d_kv[-HALF:]], axis=0)
    returned = padded(rims.astype(jnp.bfloat16), (("seq", 0),), HALF).astype(rims.dtype)
    own_grad = d_kv[HALF : HALF + rows_here]
    own_grad = own_grad + jnp.pad(returned[:HALF], ((0, rows_here - HALF), (0, 0)))
    own_grad = own_grad + jnp.pad(returned[-HALF:], ((rows_here - HALF, 0), (0, 0)))
    d_mixed = jnp.concatenate(
        [
            rotate(d_query.reshape(stream.shape), -places),
            rotate(own_grad[:, :width], -places),
            own_grad[:, width:],
        ],
        axis=1,
    ).astype(jnp.bfloat16)
    grad_qkv = inner(normed, d_mixed)
    d_normed = outer(d_mixed, w_qkv)
    in_part, gain_one = jax.vjp(layer_norm, stream, gain[0])[1](d_normed)
    d_stream = d_middle + in_part
    grad_gain = jnp.stack([gain_one, gain_two])
    return (d_stream, (grad_qkv, grad_attn, grad_in, grad_out, grad_gain))


def regroup(grad_part, along, parts_weight, parts_seq):
    shape = grad_part.shape
    length = shape[along]
    split = (
        shape[:along]
        + (parts_weight, parts_seq, length // (parts_weight * parts_seq))
        + shape[along + 1 :]
    )
    return jnp.swapaxes(grad_part.reshape(split), along, along + 1).reshape(shape)


def reduce_grads(weight_grads):
    parts_weight = lax.axis_size("weight")
    parts_seq = lax.axis_size("seq")
    ordered = tuple(
        (
            regroup(member, along, parts_weight, parts_seq)
            for member, along in zip(weight_grads, (0, 0, 0, 1, 1))
        )
    )
    summed = (
        lax.psum_scatter(ordered[0], ("seq", "weight"), scatter_dimension=0, tiled=True),
        lax.psum_scatter(ordered[1], ("seq", "weight"), scatter_dimension=0, tiled=True),
        lax.psum_scatter(ordered[2], ("seq", "weight"), scatter_dimension=0, tiled=True),
        lax.psum_scatter(ordered[3], ("seq", "weight"), scatter_dimension=1, tiled=True),
        lax.psum_scatter(ordered[4], ("seq", "weight"), scatter_dimension=1, tiled=True),
    )
    return (
        lax.all_gather(summed[0].astype(jnp.bfloat16), "seq", axis=0, tiled=True).astype(
            jnp.float32
        ),
        lax.all_gather(summed[1].astype(jnp.bfloat16), "seq", axis=0, tiled=True).astype(
            jnp.float32
        ),
        lax.all_gather(summed[2].astype(jnp.bfloat16), "seq", axis=0, tiled=True).astype(
            jnp.float32
        ),
        lax.all_gather(summed[3].astype(jnp.bfloat16), "seq", axis=1, tiled=True).astype(
            jnp.float32
        ),
        lax.all_gather(summed[4].astype(jnp.bfloat16), "seq", axis=1, tiled=True).astype(
            jnp.float32
        ),
    )


def body(
    tokens,
    cotangent,
    offsets,
    qkv_weight,
    attn_out_weight,
    mlp_in_weight,
    mlp_out_weight,
    norm_gains,
):
    layer_count = qkv_weight.shape[0]
    stream = tokens[0].astype(jnp.float32)
    bounds = offsets[0]
    rows_here = stream.shape[0]
    first_row = lax.axis_index("seq") * rows_here
    total_rows = lax.axis_size("seq") * rows_here
    query_glob = first_row + jnp.arange(rows_here, dtype=jnp.int32)
    key_glob = first_row - HALF + jnp.arange(rows_here + 2 * HALF, dtype=jnp.int32)
    places = query_glob - seq_start(query_glob, bounds)
    window = window_mask(query_glob, key_glob, bounds, total_rows)

    def pick(layer_idx):
        return (
            qkv_weight[layer_idx],
            attn_out_weight[layer_idx],
            mlp_in_weight[layer_idx],
            mlp_out_weight[layer_idx],
            norm_gains[layer_idx],
        )

    kept_weights = []
    saved_list = []
    for layer_idx in range(layer_count):
        weights = fetch_forward(pick(layer_idx))
        kept_weights.append(weights)
        stream, cache = layer_forward(stream, weights, places, window)
        saved_list.append(cache)
    output = stream.astype(jnp.bfloat16)[None]
    upstream = cotangent[0].astype(jnp.float32)
    results = [None] * layer_count
    for layer_idx in reversed(range(layer_count)):
        weights = fetch_backward(pick(layer_idx))
        upstream, weight_grads = layer_backward(
            upstream, weights, saved_list[layer_idx], places, window
        )
        results[layer_idx] = reduce_grads(weight_grads)
    stacked = tuple(
        (
            jnp.stack([results[layer_idx][member] for layer_idx in range(layer_count)])
            for member in range(5)
        )
    )
    return (output, upstream[None]) + stacked


def solution(mesh):
    return jax.shard_map(
        body,
        mesh=mesh,
        in_specs=(
            P("weight", "seq", None),
            P("weight", "seq", None),
            P("weight", None),
            P(None, "weight", None),
            P(None, "weight", None),
            P(None, "weight", None),
            P(None, None, "weight"),
            P(None, None, "weight"),
        ),
        out_specs=(
            P("weight", "seq", None),
            P("weight", "seq", None),
            P(None, "weight", None),
            P(None, "weight", None),
            P(None, "weight", None),
            P(None, None, "weight"),
            P(None, None, "weight"),
        ),
        check_vma=False,
    )
```

profile of v0, /device:TPU:0, one launch (start us, length us, event | category | flops | bytes accessed | tf_op | source)
XLA Modules:
  0.0 3245.1 jit_solution(9509431850402250600)
XLA Ops:
  55.8 73.6 %all-gather.39.cloned.1.call-done = bf16[1,1024,3072]{2,1,0:T(8,128)(2,1)} async-done(((bf16[1,256,3072]{2,1,0:T(8,128)(2,1)}), bf16[1,1024,3072]{2,1,0:T(8,128)(2,1)}) %all-gather.39.cloned.1.call-update) | async-done | bytes 6291472 | tf_op jit(solution)/shard_map/all_gather | solution.py:94
  208.6 155.4 %all-gather.43.cloned.1.call-done = bf16[1,1024,5248]{2,1,0:T(8,128)(2,1)} async-done(((bf16[1,256,5248]{2,1,0:T(8,128)(2,1)}), bf16[1,1024,5248]{2,1,0:T(8,128)(2,1)}) %all-gather.43.cloned.1.call-update) | async-done | bytes 10747920 | tf_op jit(solution)/shard_map/all_gather | solution.py:96
  390.9 72.6 %all-gather.45.cloned.1.call-done = bf16[1,2624,1024]{2,1,0:T(8,128)(2,1)} async-done(((bf16[1,2624,256]{2,1,0:T(8,128)(2,1)}), bf16[1,2624,1024]{2,1,0:T(8,128)(2,1)}) %all-gather.45.cloned.1.call-update) | async-done | bytes 5373968 | tf_op jit(solution)/shard_map/all_gather | solution.py:97
  471.3 107.2 %all-gather.47.cloned.1.call-done = bf16[1,1024,3072]{2,1,0:T(8,128)(2,1)} async-done(((bf16[1,256,3072]{2,1,0:T(8,128)(2,1)}), bf16[1,1024,3072]{2,1,0:T(8,128)(2,1)}) %all-gather.47.cloned.1.call-update) | async-done | bytes 6291472 | tf_op jit(solution)/shard_map/all_gather | solution.py:94
  658.8 154.1 %all-gather.51.cloned.1.call-done = bf16[1,1024,5248]{2,1,0:T(8,128)(2,1)} async-done(((bf16[1,256,5248]{2,1,0:T(8,128)(2,1)}), bf16[1,1024,5248]{2,1,0:T(8,128)(2,1)}) %all-gather.51.cloned.1.call-update) | async-done | bytes 10747920 | tf_op jit(solution)/shard_map/all_gather | solution.py:96
  826.2 86.3 %all-gather.53.cloned.1.call-done = bf16[1,2624,1024]{2,1,0:T(8,128)(2,1)} async-done(((bf16[1,2624,256]{2,1,0:T(8,128)(2,1)}), bf16[1,2624,1024]{2,1,0:T(8,128)(2,1)}) %all-gather.53.cloned.1.call-update) | async-done | bytes 5373968 | tf_op jit(solution)/shard_map/all_gather | solution.py:97
  912.5 18.1 fusion.77
  970.5 17.7 multiply_reduce_fusion.1
  988.3 20.5 multiply_convert_fusion.1
  1087.7 17.3 fusion.78
  1260.3 16.7 fusion.105
  1341.8 60.8 %reduce-scatter.17.cloned.1.call-done = f32[32,3072]{1,0:T(8,128)} async-done(((f32[1024,3072]{1,0:T(8,128)}), f32[32,3072]{1,0:T(8,128)}) %reduce-scatter.17.cloned.1.call-update) | async-done | bytes 393232 | tf_op jit(solution)/shard_map/reduce_scatter | solution.py:230
  1404.4 158.0 %reduce-scatter.15.cloned.1.call-done = f32[32,3072]{1,0:T(8,128)} async-done(((f32[1024,3072]{1,0:T(8,128)}), f32[32,3072]{1,0:T(8,128)}) %reduce-scatter.15.cloned.1.call-update) | async-done | bytes 393232 | tf_op jit(solution)/shard_map/reduce_scatter | solution.py:230
  1564.2 461.0 %reduce-scatter.25.cloned.1.call-done = f32[32,5248]{1,0:T(8,128)} async-done(((f32[1024,5248]{1,0:T(8,128)}), f32[32,5248]{1,0:T(8,128)}) %reduce-scatter.25.cloned.1.call-update) | async-done | bytes 671760 | tf_op jit(solution)/shard_map/reduce_scatter | solution.py:232
  2027.3 460.4 %reduce-scatter.23.cloned.1.call-done = f32[32,5248]{1,0:T(8,128)} async-done(((f32[1024,5248]{1,0:T(8,128)}), f32[32,5248]{1,0:T(8,128)}) %reduce-scatter.23.cloned.1.call-update) | async-done | bytes 671760 | tf_op jit(solution)/shard_map/reduce_scatter | solution.py:232
  2497.1 128.3 %reduce-scatter.33.cloned.1.call-done = f32[32,2]{1,0:T(8,128)} async-done(((f32[1024,2]{1,0:T(8,128)}), f32[32,2]{1,0:T(8,128)}) %reduce-scatter.33.cloned.1.call-update) | async-done | bytes 272
  2633.7 126.6 %reduce-scatter.31.cloned.1.call-done = f32[32,2]{1,0:T(8,128)} async-done(((f32[1024,2]{1,0:T(8,128)}), f32[32,2]{1,0:T(8,128)}) %reduce-scatter.31.cloned.1.call-update) | async-done | bytes 272
  2769.2 138.7 %reduce-scatter.21.cloned.1.call-done = f32[32,1024]{1,0:T(8,128)} async-done(((f32[1024,1024]{1,0:T(8,128)}), f32[32,1024]{1,0:T(8,128)}) %reduce-scatter.21.cloned.1.call-update) | async-done | bytes 131088 | tf_op jit(solution)/shard_map/reduce_scatter | solution.py:231
  2919.3 140.3 %reduce-scatter.19.cloned.1.call-done = f32[32,1024]{1,0:T(8,128)} async-done(((f32[1024,1024]{1,0:T(8,128)}), f32[32,1024]{1,0:T(8,128)}) %reduce-scatter.19.cloned.1.call-update) | async-done | bytes 131088 | tf_op jit(solution)/shard_map/reduce_scatter | solution.py:231
  3084.9 26.5 all-gather.35.cloned.1.call-done
  3122.0 16.9 all-gather.29.cloned.1.call-done
  3138.9 27.5 all-gather.27.cloned.1.call-done
  3171.4 27.2 all-gather.33.cloned.1.call-done
  3198.5 32.0 all-gather.31.cloned.1.call-done
  (509 shorter events, 685.1 us)
Async XLA Ops:
  7.2 122.2 %all-gather.39.cloned.1.call-start = ((), (), s32[]{:S(2)}) async-start(), calls=%async_computation.24 | async-start | bytes 7864320 | tf_op jit(solution)/shard_map/all_gather | solution.py:94
  11.1 192.6 %all-gather.41.cloned.1.call-start = ((), (), s32[]{:S(2)}) async-start(), calls=%async_computation.25 | async-start | bytes 2621440 | tf_op jit(solution)/shard_map/all_gather | solution.py:95
  12.2 351.8 %all-gather.43.cloned.1.call-start = ((), (), s32[]{:S(2)}) async-start(), calls=%async_computation.26 | async-start | bytes 13434880 | tf_op jit(solution)/shard_map/all_gather | solution.py:96
  17.8 445.7 %all-gather.45.cloned.1.call-start = ((), (), s32[]{:S(2)}) async-start(), calls=%async_computation.27 | async-start | bytes 6717440 | tf_op jit(solution)/shard_map/all_gather | solution.py:97
  19.6 558.9 %all-gather.47.cloned.1.call-start = ((), (), s32[]{:S(2)}) async-start(), calls=%async_computation.28 | async-start | bytes 7864320 | tf_op jit(solution)/shard_map/all_gather | solution.py:94
  20.2 633.7 %all-gather.49.cloned.1.call-start = ((), (), s32[]{:S(2)}) async-start(), calls=%async_computation.29 | async-start | bytes 2621440 | tf_op jit(solution)/shard_map/all_gather | solution.py:95
  20.7 792.2 %all-gather.51.cloned.1.call-start = ((), (), s32[]{:S(2)}) async-start(), calls=%async_computation.30 | async-start | bytes 13434880 | tf_op jit(solution)/shard_map/all_gather | solution.py:96
  21.5 891.0 %all-gather.53.cloned.1.call-start = ((), (), s32[]{:S(2)}) async-start(), calls=%async_computation.31 | async-start | bytes 6717440 | tf_op jit(solution)/shard_map/all_gather | solution.py:97
  22.2 1316.0 %reduce-scatter.29.cloned.1.call-start = ((), (), s32[]{:S(2)}) async-start(), calls=%async_computation.22 | async-start | bytes 11354112 | tf_op jit(solution)/shard_map/reduce_scatter | solution.py:233
  945.8 394.3 %reduce-scatter.27.cloned.1.call-start = ((), (), s32[]{:S(2)}) async-start(), calls=%async_computation.20 | async-start | bytes 11354112 | tf_op jit(solution)/shard_map/reduce_scatter | solution.py:233
  1061.9 340.8 %reduce-scatter.17.cloned.1.call-start = ((), (), s32[]{:S(2)}) async-start(), calls=%async_computation.12 | async-start | bytes 12976128 | tf_op jit(solution)/shard_map/reduce_scatter | solution.py:230
  1087.6 474.8 %reduce-scatter.15.cloned.1.call-start = ((), (), s32[]{:S(2)}) async-start(), calls=%async_computation.10 | async-start | bytes 12976128 | tf_op jit(solution)/shard_map/reduce_scatter | solution.py:230
  1259.7 765.5 %reduce-scatter.25.cloned.1.call-start = ((), (), s32[]{:S(2)}) async-start(), calls=%async_computation.18 | async-start | bytes 22167552 | tf_op jit(solution)/shard_map/reduce_scatter | solution.py:232
  1293.3 1194.4 %reduce-scatter.23.cloned.1.call-start = ((), (), s32[]{:S(2)}) async-start(), calls=%async_computation.16 | async-start | bytes 22167552 | tf_op jit(solution)/shard_map/reduce_scatter | solution.py:232
  1325.1 1300.2 %reduce-scatter.33.cloned.1.call-start = ((), (), s32[]{:S(2)}) async-start(), calls=%async_computation.33 | async-start | bytes 540672
  1327.1 1433.2 %reduce-scatter.31.cloned.1.call-start = ((), (), s32[]{:S(2)}) async-start(), calls=%async_computation.32 | async-start | bytes 540672
  1328.3 1579.6 %reduce-scatter.21.cloned.1.call-start = ((), (), s32[]{:S(2)}) async-start(), calls=%async_computation.15 | async-start | bytes 4325376 | tf_op jit(solution)/shard_map/reduce_scatter | solution.py:231
  1333.2 1726.3 %reduce-scatter.19.cloned.1.call-start = ((), (), s32[]{:S(2)}) async-start(), calls=%async_computation.14 | async-start | bytes 4325376 | tf_op jit(solution)/shard_map/reduce_scatter | solution.py:231
  1338.1 1746.7 %all-gather.37.cloned.1.call-start = ((), (), s32[]{:S(2)}) async-start(), calls=%async_computation.23 | async-start | bytes 1548288 | tf_op jit(solution)/shard_map/all_gather | solution.py:246
  1340.0 1771.4 %all-gather.35.cloned.1.call-start = ((), (), s32[]{:S(2)}) async-start(), calls=%async_computation.21 | async-start | bytes 1548288 | tf_op jit(solution)/shard_map/all_gather | solution.py:246
  1341.8 1797.1 %all-gather.29.cloned.1.call-start = ((), (), s32[]{:S(2)}) async-start(), calls=%async_computation.13 | async-start | bytes 1769472 | tf_op jit(solution)/shard_map/all_gather | solution.py:237
  1404.4 1762.0 %all-gather.27.cloned.1.call-start = ((), (), s32[]{:S(2)}) async-start(), calls=%async_computation.11 | async-start | bytes 1769472 | tf_op jit(solution)/shard_map/all_gather | solution.py:237
  1564.2 1634.4 %all-gather.33.cloned.1.call-start = ((), (), s32[]{:S(2)}) async-start(), calls=%async_computation.19 | async-start | bytes 3022848 | tf_op jit(solution)/shard_map/all_gather | solution.py:243
  2027.1 1203.5 %all-gather.31.cloned.1.call-start = ((), (), s32[]{:S(2)}) async-start(), calls=%async_computation.17 | async-start | bytes 3022848 | tf_op jit(solution)/shard_map/all_gather | solution.py:243
  (130 other events, 4650.3 us)
Sparse Core Ops, SparseCore 0:
  11.2 118.1 all-gather.38
  131.0 43.8 all-gather.40
  177.0 186.9 all-gather.42
  365.4 97.9 all-gather.44
  464.9 113.5 all-gather.46
  579.9 43.8 all-gather.48
  625.9 186.9 all-gather.50
  814.5 97.9 all-gather.52
  945.9 146.2 reduce-scatter.28
  1098.0 144.6 reduce-scatter.26
  1248.8 153.8 reduce-scatter.16
  1408.6 153.8 reduce-scatter.14
  1564.7 460.4 reduce-scatter.24
  2027.4 460.2 reduce-scatter.22
  2490.4 134.9 reduce-scatter.32
  2628.1 132.2 reduce-scatter.30
  2763.0 144.8 reduce-scatter.20
  2910.6 148.8 reduce-scatter.18
  3061.4 23.4 all-gather.36
  3086.6 24.7 all-gather.34
  3113.3 25.5 all-gather.28
  3140.8 25.5 all-gather.26
  3168.2 30.2 all-gather.32
  3200.3 30.2 all-gather.30
where the time goes:
time: 3250 us
  waiting for transfers between devices  2470 us (76%)
  matrix products  313 us (10%)
  local copies, waits for them, and re-layouts  206 us (6%)
  other arithmetic  158 us (5%)
  blocking collectives  58.8 us (2%)
    reduce_scatter x2, waiting for transfers between devices, reduce_grads(): lax.psum_scatter(ordered[2], ('seq', 'weight'), scatter_dimension=0, tile...  921 us
    all_gather x2, waiting for transfers between devices, fetch_forward(): lax.all_gather(pieces[2], 'weight', axis=0, tiled=True)  309 us
    reduce_scatter x2, waiting for transfers between devices, reduce_grads(): lax.psum_scatter(ordered[1], ('seq', 'weight'), scatter_dimension=0, tile...  279 us
    unnamed x26, waiting for transfers between devices  258 us
    reduce_scatter x2, waiting for transfers between devices, reduce_grads(): lax.psum_scatter(ordered[0], ('seq', 'weight'), scatter_dimension=0, tile...  219 us
    all_gather x2, waiting for transfers between devices, fetch_forward(): lax.all_gather(pieces[0], 'weight', axis=0, tiled=True)  181 us
    all_gather x2, waiting for transfers between devices, fetch_forward(): lax.all_gather(pieces[3], 'weight', axis=1, tiled=True)  159 us
    dot_general x8, matrix products, outer(): lax.dot_general(left, right, (((1,), (1,)), ((), ())), preferred_element_...  79.9 us
  transfers between devices with their start and end apart: 32, of which 21 were waited for; matrix products, arithmetic and copies ran while one was open for 18% of the time, Pallas kernels for 0%

commit v1 on v0

--- a/solution.py
+++ b/solution.py
@@ -1,6 +1,8 @@
 import jax
 import jax.numpy as jnp
 from jax import lax
+from jax.experimental import pallas as pl
+from jax.experimental.pallas import tpu as pltpu
 from jax.sharding import PartitionSpec as P
 
 HEADS = 16
@@ -89,32 +91,218 @@
     return jnp.where(window[None], raw * HEAD_DIM ** (-0.5), NEG)
 
 
-def fetch_forward(pieces):
-    return (
-        lax.all_gather(pieces[0], "weight", axis=0, tiled=True),
-        lax.all_gather(pieces[1], "weight", axis=0, tiled=True),
-        lax.all_gather(pieces[2], "weight", axis=0, tiled=True),
-        lax.all_gather(pieces[3], "weight", axis=1, tiled=True),
-        lax.all_gather(pieces[4], "weight", axis=1, tiled=True),
-    )
-
-
-def fetch_backward(pieces):
-    return (
-        lax.all_gather(pieces[0], "weight", axis=0, tiled=True),
-        lax.all_gather(pieces[1], "weight", axis=0, tiled=True),
-        lax.all_gather(pieces[2], "weight", axis=0, tiled=True),
-        lax.all_gather(pieces[3], "weight", axis=1, tiled=True),
-        lax.all_gather(pieces[4], "weight", axis=1, tiled=True),
-    )
-
-
-def layer_forward(stream, weights, places, window):
-    w_qkv, w_attn, w_in, w_out, gain_low = weights
+LANES = 128
+
+
+def pad_lanes(values):
+    extra = -values.shape[-1] % LANES
+    return jnp.pad(values, ((0, 0),) * (values.ndim - 1) + ((0, extra),))
+
+
+def seq_swap(values, bit):
+    count = lax.axis_size("seq")
+    return lax.ppermute(values, "seq", [(i, i ^ bit) for i in range(count)])
+
+
+def chip_orders(pieces):
+    bits = [1 << k for k in range(1, lax.axis_size("seq").bit_length() - 1)]
+    return [bits[p % len(bits) :] + bits[: p % len(bits)] for p in range(pieces)]
+
+
+def part_bounds(total, parts):
+    edges = [total * p // parts for p in range(parts + 1)]
+    return list(zip(edges[:-1], edges[1:]))
+
+
+def spread(part, order):
+    held = {0: part}
+    for bit in order:
+        held.update({mask ^ bit: seq_swap(piece, bit) for mask, piece in list(held.items())})
+    return held
+
+
+def assemble_kernel(index_ref, *refs, plan, count_in, count_out):
+    sources = refs[:count_in]
+    targets = refs[count_in : count_in + count_out]
+    sems = refs[-1]
+    index = index_ref[0]
+    copies = []
+    for number, (mask, low, high) in enumerate(plan):
+        place = jnp.bitwise_xor(index, mask)
+        column = 0
+        for which, target in enumerate(targets):
+            wide = target.shape[-1]
+            copies.append(
+                pltpu.make_async_copy(
+                    sources[number].at[:, :, column : column + wide],
+                    target.at[low:high, place],
+                    sems.at[number, which],
+                )
+            )
+            column += wide
+    for copy in copies:
+        copy.start()
+    for copy in copies:
+        copy.wait()
+
+
+def assemble(index, parts, widths):
+    count = lax.axis_size("seq")
+    plan, sources = [], []
+    for low, high, held in parts:
+        for mask, piece in held.items():
+            plan.append((mask, low, high))
+            sources.append(piece)
+    lead = parts[-1][1]
+    rows = sources[0].shape[1]
+    kind = sources[0].dtype
+
+    def kernel(*refs):
+        assemble_kernel(*refs, plan=plan, count_in=len(sources), count_out=len(widths))
+
+    anywhere = pl.BlockSpec(memory_space=pl.ANY)
+    return pl.pallas_call(
+        kernel,
+        out_shape=[jax.ShapeDtypeStruct((lead, count, rows, wide), kind) for wide in widths],
+        grid_spec=pltpu.PrefetchScalarGridSpec(
+            num_scalar_prefetch=1,
+            grid=(),
+            in_specs=[anywhere] * len(sources),
+            out_specs=[pl.BlockSpec(memory_space=pltpu.VMEM)] * len(widths),
+            scratch_shapes=[pltpu.SemaphoreType.DMA((len(plan), len(widths)))],
+        ),
+        name="assemble",
+    )(index.reshape(1), *sources)
+
+
+def line_up(columns):
+    index = lax.axis_index("seq")
+    rows = columns[0].shape[0] // lax.axis_size("seq")
+    own = jnp.concatenate(
+        [lax.dynamic_slice_in_dim(member, index * rows, rows, 0) for member in columns], axis=1
+    )
+    return lax.all_gather(own, "weight", axis=0, tiled=False)
+
+
+def fill_out(line, widths):
+    groups, rows, _ = line.shape
+    count = lax.axis_size("seq")
+    orders = chip_orders(min(groups, max(1, count.bit_length() - 2)))
+    parts = [
+        (low, high, spread(line[low:high], order + [1]))
+        for (low, high), order in zip(part_bounds(groups, len(orders)), orders)
+    ]
+    whole = assemble(lax.axis_index("seq"), parts, widths)
+    return [member.reshape(groups * count * rows, -1) for member in whole]
+
+
+def fetch_start(pieces):
+    w_qkv, w_attn, w_in, w_out, gain_low = pieces
+    width = w_in.shape[1] // 2
+    first = [w_qkv, w_attn, pad_lanes(gain_low.T)]
+    second = [
+        jnp.concatenate([pad_lanes(w_in[:, :width]), pad_lanes(w_in[:, width:])], axis=1),
+        pad_lanes(w_out.T),
+    ]
+    return tuple((line_up(some), [member.shape[1] for member in some]) for some in (first, second))
+
+
+def fetch_first(line, widths):
+    full_qkv, full_attn, full_gain = fill_out(line, widths)
+    return full_qkv, full_attn, full_gain[:, :2].T
+
+
+def fetch_second(line, widths):
+    return tuple(fill_out(line, widths))
+
+
+def sum_grads(members):
+    index = lax.axis_index("seq")
+    count = lax.axis_size("seq")
+    groups = lax.axis_size("weight")
+    rows = members[0].shape[0] // (count * groups)
+    bits = count.bit_length() - 2
+
+    def side(bit):
+        return (index // bit) % 2
+
+    def half(values, axis, which):
+        return lax.dynamic_index_in_dim(values, which, axis, keepdims=False)
+
+    split = [m.reshape((groups,) + (2,) * (bits + 1) + (rows, m.shape[1])) for m in members]
+    send = jnp.concatenate([half(m, bits + 1, 1 - side(1)) for m in split], axis=-1)
+    keep = jnp.concatenate([half(m, bits + 1, side(1)) for m in split], axis=-1)
+    got = yield seq_swap(send, 1)
+    total = keep + got
+    orders = chip_orders(min(groups, max(1, bits)))
+    bounds = part_bounds(groups, len(orders))
+    parts = [total[low:high] for low, high in bounds]
+    left = [[1 << k for k in range(bits, 0, -1)] for _ in parts]
+    for step in range(bits):
+        axes = [1 + rest.index(order[step]) for rest, order in zip(left, orders)]
+        for rest, order in zip(left, orders):
+            rest.remove(order[step])
+        got = yield [
+            seq_swap(half(part, axis, 1 - side(order[step])), order[step])
+            for part, axis, order in zip(parts, axes, orders)
+        ]
+        parts = [
+            half(part, axis, side(order[step])) + more
+            for part, axis, order, more in zip(parts, axes, orders, got)
+        ]
+    line = jnp.concatenate(parts, axis=0).reshape(groups * rows, -1)
+    own = lax.psum_scatter(line, "weight", scatter_dimension=0, tiled=True)
+    yield None
+    own = yield own
+    held = {0: own[None]}
+    for bit in chip_orders(1)[0] + [1]:
+        masks = list(held)
+        got = yield [seq_swap(held[mask], bit) for mask in masks]
+        held.update({mask ^ bit: more for mask, more in zip(masks, got)})
+    whole = assemble(index, [(0, 1, held)], [m.shape[1] for m in members])
+    return [m.reshape(count * rows, -1) for m in whole]
+
+
+class Sums:
+    def __init__(self):
+        self.active = []
+        self.done = {}
+
+    def add(self, key, members):
+        chain = sum_grads(members)
+        self.active.append((key, chain, next(chain)))
+
+    def step(self, flights):
+        after = []
+        for (key, chain, _), flight in zip(self.active, flights):
+            try:
+                after.append((key, chain, chain.send(flight)))
+            except StopIteration as end:
+                self.done[key] = end.value
+        self.active = after
+
+    def tie(self, value):
+        value, flights = lax.optimization_barrier((value, [entry[2] for entry in self.active]))
+        self.step(flights)
+        return value
+
+    def finish(self):
+        while self.active:
+            self.step([entry[2] for entry in self.active])
+
+
+def layer_forward(stream, lines, ahead, places, window):
+    (first_line, first_widths), (second_line, second_widths) = lines
+    w_qkv, w_attn, gain_low = fetch_first(first_line, first_widths)
+    w_in, w_out = fetch_second(second_line, second_widths)
+    next_lines = None
     gain = gain_low.astype(jnp.float32)
     width = stream.shape[1]
     normed = layer_norm(stream, gain[0]).astype(jnp.bfloat16)
     mixed = jnp.dot(normed, w_qkv, preferred_element_type=jnp.float32)
+    if ahead is not None:
+        (next_first, widths_one), (next_second, widths_two) = ahead
+        mixed, next_first = lax.optimization_barrier((mixed, next_first))
     queries = rotate(mixed[:, :width], places).astype(jnp.bfloat16)
     keys = rotate(mixed[:, width : 2 * width], places).astype(jnp.bfloat16)
     values = mixed[:, 2 * width :].astype(jnp.bfloat16)
@@ -127,18 +315,23 @@
         "hqk,khd->qhd", prob, split_heads(kv_wide[:, width:]), preferred_element_type=jnp.float32
     )
     context = context.reshape(stream.shape).astype(jnp.bfloat16)
+    if ahead is not None:
+        context, next_second = lax.optimization_barrier((context, next_second))
+        next_lines = ((next_first, widths_one), (next_second, widths_two))
     middle = stream + jnp.dot(context, w_attn, preferred_element_type=jnp.float32)
     shaped = layer_norm(middle, gain[1]).astype(jnp.bfloat16)
     gate_up = jnp.dot(shaped, w_in, preferred_element_type=jnp.float32)
     hidden = geglu(gate_up).astype(jnp.bfloat16)
-    result = middle + jnp.dot(hidden, w_out, preferred_element_type=jnp.float32)
+    result = middle + outer(hidden, w_out)
     return (
         result,
+        next_lines,
+        (w_qkv, w_attn, w_in, w_out, gain_low),
         (stream, normed, queries, kv_wide, log_total, context, middle, shaped, gate_up, hidden),
     )
 
 
-def layer_backward(upstream, weights, saved_acts, places, window):
+def layer_backward(upstream, weights, saved_acts, places, window, sums, layer_idx):
     w_qkv, w_attn, w_in, w_out, gain_low = weights
     gain = gain_low.astype(jnp.float32)
     stream, normed, queries, kv_wide, log_total, context, middle, shaped, gate_up, hidden = (
@@ -147,16 +340,19 @@
     width = stream.shape[1]
     rows_here = stream.shape[0]
     up_low = upstream.astype(jnp.bfloat16)
-    grad_out = inner(hidden, up_low)
-    d_hidden = outer(up_low, w_out)
+    grad_out = inner(up_low, hidden).astype(jnp.bfloat16)
+    sums.add((layer_idx, "out"), [grad_out])
+    d_hidden = jnp.dot(up_low, w_out, preferred_element_type=jnp.float32)
     d_gate_up = jax.vjp(geglu, gate_up)[1](d_hidden)[0].astype(jnp.bfloat16)
-    grad_in = inner(shaped, d_gate_up)
+    d_gate_up = sums.tie(d_gate_up)
+    grad_in = inner(shaped, d_gate_up).astype(jnp.bfloat16)
+    sums.add((layer_idx, "in"), [grad_in])
     d_shaped = outer(d_gate_up, w_in)
     mid_part, gain_two = jax.vjp(layer_norm, middle, gain[1])[1](d_shaped)
-    d_middle = upstream + mid_part
+    d_middle = sums.tie(upstream + mid_part)
     mid_low = d_middle.astype(jnp.bfloat16)
-    grad_attn = inner(context, mid_low)
-    d_context = outer(mid_low, w_attn).astype(jnp.bfloat16)
+    grad_attn = inner(context, mid_low).astype(jnp.bfloat16)
+    d_context = sums.tie(outer(mid_low, w_attn).astype(jnp.bfloat16))
     key_wide = kv_wide[:, :width]
     value_wide = kv_wide[:, width:]
     prob = jnp.exp(attn_scores(queries, key_wide, window) - log_total)
@@ -182,6 +378,7 @@
     d_value = jnp.einsum(
         "hqk,qhd->khd", prob.astype(jnp.bfloat16), context_heads, preferred_element_type=jnp.float32
     )
+    d_key, d_value = sums.tie((d_key, d_value))
     d_kv = jnp.concatenate(
         [d_key.reshape(key_wide.shape), d_value.reshape(value_wide.shape)], axis=1
     )
@@ -198,58 +395,16 @@
         ],
         axis=1,
     ).astype(jnp.bfloat16)
-    grad_qkv = inner(normed, d_mixed)
+    d_mixed = sums.tie(d_mixed)
+    grad_qkv = inner(normed, d_mixed).astype(jnp.bfloat16)
     d_normed = outer(d_mixed, w_qkv)
     in_part, gain_one = jax.vjp(layer_norm, stream, gain[0])[1](d_normed)
     d_stream = d_middle + in_part
-    grad_gain = jnp.stack([gain_one, gain_two])
-    return (d_stream, (grad_qkv, grad_attn, grad_in, grad_out, grad_gain))
-
-
-def regroup(grad_part, along, parts_weight, parts_seq):
-    shape = grad_part.shape
-    length = shape[along]
-    split = (
-        shape[:along]
-        + (parts_weight, parts_seq, length // (parts_weight * parts_seq))
-        + shape[along + 1 :]
-    )
-    return jnp.swapaxes(grad_part.reshape(split), along, along + 1).reshape(shape)
-
-
-def reduce_grads(weight_grads):
-    parts_weight = lax.axis_size("weight")
-    parts_seq = lax.axis_size("seq")
-    ordered = tuple(
-        (
-            regroup(member, along, parts_weight, parts_seq)
-            for member, along in zip(weight_grads, (0, 0, 0, 1, 1))
-        )
-    )
-    summed = (
-        lax.psum_scatter(ordered[0], ("seq", "weight"), scatter_dimension=0, tiled=True),
-        lax.psum_scatter(ordered[1], ("seq", "weight"), scatter_dimension=0, tiled=True),
-        lax.psum_scatter(ordered[2], ("seq", "weight"), scatter_dimension=0, tiled=True),
-        lax.psum_scatter(ordered[3], ("seq", "weight"), scatter_dimension=1, tiled=True),
-        lax.psum_scatter(ordered[4], ("seq", "weight"), scatter_dimension=1, tiled=True),
-    )
-    return (
-        lax.all_gather(summed[0].astype(jnp.bfloat16), "seq", axis=0, tiled=True).astype(
-            jnp.float32
-        ),
-        lax.all_gather(summed[1].astype(jnp.bfloat16), "seq", axis=0, tiled=True).astype(
-            jnp.float32
-        ),
-        lax.all_gather(summed[2].astype(jnp.bfloat16), "seq", axis=0, tiled=True).astype(
-            jnp.float32
-        ),
-        lax.all_gather(summed[3].astype(jnp.bfloat16), "seq", axis=1, tiled=True).astype(
-            jnp.float32
-        ),
-        lax.all_gather(summed[4].astype(jnp.bfloat16), "seq", axis=1, tiled=True).astype(
-            jnp.float32
-        ),
-    )
+    grad_gain = pad_lanes(jnp.stack([gain_one, gain_two], axis=1)).astype(jnp.bfloat16)
+    sums.add((layer_idx, "rest"), [grad_qkv, grad_attn, grad_gain])
+    if layer_idx:
+        d_stream = sums.tie(d_stream)
+    return d_stream
 
 
 def body(
@@ -284,27 +439,51 @@
 
     kept_weights = []
     saved_list = []
+    lines = [fetch_start(pick(layer_idx)) for layer_idx in range(layer_count)]
+    ready = lines[0]
     for layer_idx in range(layer_count):
-        weights = fetch_forward(pick(layer_idx))
+        ahead = lines[layer_idx + 1] if layer_idx + 1 < layer_count else None
+        stream, ready, weights, cache = layer_forward(stream, ready, ahead, places, window)
         kept_weights.append(weights)
-        stream, cache = layer_forward(stream, weights, places, window)
         saved_list.append(cache)
     output = stream.astype(jnp.bfloat16)[None]
     upstream = cotangent[0].astype(jnp.float32)
-    results = [None] * layer_count
+    sums = Sums()
     for layer_idx in reversed(range(layer_count)):
-        weights = fetch_backward(pick(layer_idx))
-        upstream, weight_grads = layer_backward(
-            upstream, weights, saved_list[layer_idx], places, window
+        upstream = layer_backward(
+            upstream,
+            kept_weights[layer_idx],
+            saved_list[layer_idx],
+            places,
+            window,
+            sums,
+            layer_idx,
         )
-        results[layer_idx] = reduce_grads(weight_grads)
-    stacked = tuple(
-        (
-            jnp.stack([results[layer_idx][member] for layer_idx in range(layer_count)])
-            for member in range(5)
-        )
-    )
-    return (output, upstream[None]) + stacked
+    sums.finish()
+    results = []
+    for layer_idx in range(layer_count):
+        (sum_out,), (sum_in,) = sums.done[layer_idx, "out"], sums.done[layer_idx, "in"]
+        sum_qkv, sum_attn, sum_gain = sums.done[layer_idx, "rest"]
+        results.append((sum_qkv, sum_attn, sum_in, sum_out, sum_gain))
+    hidden_width = mlp_in_weight.shape[2] // 2
+    padded_width = hidden_width + -hidden_width % LANES
+
+    def finish(member):
+        return jnp.stack([results[layer_idx][member] for layer_idx in range(layer_count)])
+
+    sum_in = finish(2)
+    return (
+        output,
+        upstream[None],
+        finish(0).astype(jnp.float32),
+        finish(1).astype(jnp.float32),
+        jnp.concatenate(
+            [sum_in[..., :hidden_width], sum_in[..., padded_width : padded_width + hidden_width]],
+            axis=2,
+        ).astype(jnp.float32),
+        jnp.swapaxes(finish(3)[..., :hidden_width], 1, 2).astype(jnp.float32),
+        jnp.swapaxes(finish(4)[..., :2], 1, 2).astype(jnp.float32),
+    )
 
 
 def solution(mesh):

time: 3250 us -> 1200 us (0.37)
  waiting for transfers between devices: 2470 us -> 329 us
  starting transfers between devices: 22.7 us -> 131 us
  blocking collectives: 58.8 us -> 0 us
  Pallas kernels: 0 us -> 57.1 us
  other arithmetic: 158 us -> 212 us
  matrix products: 313 us -> 268 us
    reduce_scatter x8 -> x6, waiting for transfers between devices: 1420 us -> 25.9 us  [sum_grads(): own = lax.psum_scatter(line, 'weight', scatter_dimension=0, tiled=True)]
    all_gather x14 -> x4, waiting for transfers between devices: 793 us -> 24.1 us  [line_up(): return lax.all_gather(own, 'weight', axis=0, tiled=False)]
    ppermute x0 -> x128, waiting for transfers between devices: none -> 279 us  [seq_swap(): return lax.ppermute(values, 'seq', [(i, i ^ bit) for i in range(count)])]
    unnamed x26 -> x10, waiting for transfers between devices: 258 us -> 0.16 us
    ppermute x0 -> x128, starting transfers between devices: none -> 107 us  [seq_swap(): return lax.ppermute(values, 'seq', [(i, i ^ bit) for i in range(count)])]
    transpose x8 -> x2, local copies, waits for them, and re-layouts: 68.6 us -> 1.94 us  [the longest x1 1.24 us: fetch_start(): second = [jnp.concatenate([pad_lanes(w_in[:, :width]), pad_lanes(w_in[:,...]
    all_gather x6 -> x0, blocking collectives: 58.8 us -> none  [the longest x2 24.2 us: fetch_forward(): lax.all_gather(pieces[4], 'weight', axis=1, tiled=True)]
    pallas_call x0 -> x10, Pallas kernels: none -> 57.1 us  [assemble(): pl.pallas_call(kernel, out_shape=[jax.ShapeDtypeStruct((lead, count, rows...]
  transfers between devices with their start and end apart: 32 -> 146, of which waited for: 21 -> 39; matrix products, arithmetic and copies ran while one was open for 18% -> 35% of each run, Pallas kernels for 0% -> 3%
where the time goes in v1:
time: 1200 us; the launch traced here: 1190 us
  waiting for transfers between devices  329 us (27%)
  matrix products  268 us (22%)
  other arithmetic  212 us (18%)
  local copies, waits for them, and re-layouts  175 us (15%)
  starting transfers between devices  131 us (11%)
  Pallas kernels  57.1 us (5%)
  between operations  18 us (2%)
    ppermute x128, waiting for transfers between devices, seq_swap(): return lax.ppermute(values, 'seq', [(i, i ^ bit) for i in range(count)])  279 us
    ppermute x128, starting transfers between devices, seq_swap(): return lax.ppermute(values, 'seq', [(i, i ^ bit) for i in range(count)])  107 us
    pallas_call x10, Pallas kernels, assemble(): pl.pallas_call(kernel, out_shape=[jax.ShapeDtypeStruct((lead, count, rows...  57.1 us
    dot_general x8, matrix products, outer(): lax.dot_general(left, right, (((1,), (1,)), ((), ())), preferred_element_...  51.8 us
    unnamed x440, local copies, waits for them, and re-layouts  42.2 us
    dot_general x8, matrix products, inner(): lax.dot_general(left, right, (((0,), (0,)), ((), ())), preferred_element_...  38.6 us
    convert_element_type x2, other arithmetic, layer_backward(): d_score = (prob * (d_prob - delta)).astype(jnp.bfloat16)  34.9 us
    dot_general x2, matrix products, layer_backward(): jnp.einsum('qhd,khd->hqk', context_heads, split_heads(value_wide), prefer...  34.3 us
  transfers between devices with their start and end apart: 146, of which 39 were waited for; matrix products, arithmetic and copies ran while one was open for 35% of the time, Pallas kernels for 3%

profile of v1, /device:TPU:0, one launch (start us, length us, event | category | flops | bytes accessed | tf_op | source)
XLA Modules:
  0.0 1190.1 jit_solution(2289506171512363749)
XLA Ops:
  32.8 13.0 %all-gather.9.cloned.1.call-done = bf16[128,4224]{1,0:T(8,128)(2,1)} async-done(((bf16[32,4224]{1,0:T(8,128)(2,1)}), bf16[128,4224]{1,0:T(8,128)(2,1)}) %all-gather.9.cloned.1.call-update) | async-done | bytes 1081360 | tf_op jit(solution)/shard_map/all_gather | solution.py:184
  66.2 10.1 collective-permute-done.7.refs_10_
  183.4 27.0 %collective-permute-done.37.refs_10_ = bf16[2,32,4224]{2,1,0:T(8,128)(2,1)} collective-permute-done((bf16[2,32,4224]{2,1,0:T(8,128)(2,1)S(1)}, bf16[2,32,4224]{2,1,0:T(8,128)(2,1)}, u32[]{:S(2)}, u32[]{:S(2)}) %collective-permute-start.37) | collective-permute-done | bytes 540704 | tf_op jit(solution)/shard_map/ppermute | solution.py:104
  224.1 12.3 %collective-permute-done.23.refs_10_ = bf16[2,32,8064]{2,1,0:T(8,128)(2,1)} collective-permute-done((bf16[2,32,8064]{2,1,0:T(8,128)(2,1)}, bf16[2,32,8064]{2,1,0:T(8,128)(2,1)}, u32[]{:S(2)}, u32[]{:S(2)}) %collective-permute-start.23) | collective-permute-done | bytes 1032224 | tf_op jit(solution)/shard_map/ppermute | solution.py:104
  256.9 10.8 convolution_convert_fusion.11
  290.7 11.8 assemble.11
  311.2 13.2 %multiply_convert_fusion.3 = (bf16[512,2688]{1,0:T(8,128)(2,1)S(1)}, f32[512,2688]{1,0:T(8,128)}) fusion(f32[512,5376]{1,0:T(8,128)S(1)} %fusion.107), kind=kLoop, calls=%fused_computation.58 | loop fusion | flops 90832896 | bytes 19267584 | tf_op jit(solution)/shard_map/convert_element_type | solution.py:324
  391.6 20.4 %collective-permute-done.53.refs_10_ = bf16[2,32,8064]{2,1,0:T(8,128)(2,1)} collective-permute-done((bf16[2,32,8064]{2,1,0:T(8,128)(2,1)}, bf16[2,32,8064]{2,1,0:T(8,128)(2,1)}, u32[]{:S(2)}, u32[]{:S(2)}) %collective-permute-start.53) | collective-permute-done | bytes 1032224 | tf_op jit(solution)/shard_map/ppermute | solution.py:104
  422.8 11.1 collective-permute-done.48.refs_4_
  441.9 11.6 assemble.13
  462.3 17.2 %bitcast_multiply_fusion.1 = (f32[512,2688]{1,0:T(8,128)}, f32[512,2688]{1,0:T(8,128)S(1)}, f32[2688,512]{0,1:T(8,128)S(1)}) fusion(f32[512,5376]{1,0:T(8,128)S(1)} %fusion.109, bf16[1024,2688]{1,0:T(8,128)(2,1)} %bitcast.548, bf16[1,512,1024]{2,1,0:T(8,128)(2,1)S(1)} %copy-done.114), kind=kOutput, calls=%fused_computation.40 | convolution fusion | flops 2908028928 | bytes 28573696 | tf_op jit(solution)/shard_map/dot_general | solution.py:345
  559.3 27.2 %collective-permute-done.65 = bf16[2,32,2688]{2,1,0:T(8,128)(2,1)S(1)} collective-permute-done((bf16[2,32,2688]{2,1,0:T(8,128)(2,1)S(1)}, bf16[2,32,2688]{2,1,0:T(8,128)(2,1)S(1)}, u32[]{:S(2)}, u32[]{:S(2)}) %collective-permute-start.65) | collective-permute-done | bytes 344096 | tf_op jit(solution)/shard_map/ppermute | solution.py:104
  589.1 17.0 %multiply_reduce_fusion.1 = (f32[16,512]{1,0:T(8,128)S(1)}, f32[16,512,640]{2,1,0:T(8,128)}) fusion(f32[16,512,640]{2,1,0:T(8,128)} %copy-done.1, f32[16,512]{1,0:T(8,128)S(1)} %log_add_fusion, pred[512,640]{1,0:T(8,128)(4,1)S(1)} %fusion.58, bf16[512,16,64]{0,2,1:T(8,128)(2,1)S(1)} %bitcast.468, bf16[640,16,64]{0,2,1:T(8,128)(2,1)S(1)} %bitcast.463), kind=kOutput, calls=%fused_computation.3 | convolution fusion | flops 697294848 | bytes 44695552 | tf_op jit(solution)/shard_map/qhd,khd->hqk/dot_general | solution.py:360
  606.2 12.6 %convolution_bitcast_fusion.1 = f32[640,16,64]{0,2,1:T(8,128)} fusion(bf16[512,16,64]{0,2,1:T(8,128)(2,1)S(1)} %bitcast.469, f32[16,512,640]{2,1,0:T(8,128)} %copy-done.1, f32[16,512]{1,0:T(8,128)S(1)} %log_add_fusion, pred[512,640]{1,0:T(8,128)(4,1)S(1)} %fusion.58), kind=kOutput, calls=%fused_computation.189 | convolution fusion | flops 692060160 | bytes 25001984 | tf_op jit(solution)/shard_map/hqk,qhd->khd/dot_general | solution.py:378
  626.2 14.8 %multiply_convert_fusion.1 = bf16[16,512,640]{2,1,0:T(8,128)(2,1)} fusion(f32[16,512,640]{2,1,0:T(8,128)} %get-tuple-element.324, f32[16,512,640]{2,1,0:T(8,128)S(1)} %bitcast.410, f32[16,512]{1,0:T(8,128)S(1)} %get-tuple-element.323, f32[16,512]{1,0:T(8,128)S(1)} %log_add_fusion, pred[512,640]{1,0:T(8,128)(4,1)S(1)} %fusion.58), kind=kLoop, calls=%fused_computation.2 | loop fusion | flops 31457280 | bytes 52822016 | tf_op jit(solution)/shard_map/convert_element_type | solution.py:364
  713.6 24.9 %reduce-scatter.9.cloned.1.call-done = bf16[32,5376]{1,0:T(8,128)(2,1)} async-done(((bf16[128,5376]{1,0:T(8,128)(2,1)}), bf16[32,5376]{1,0:T(8,128)(2,1)}) %reduce-scatter.9.cloned.1.call-update) | async-done | bytes 344080 | tf_op jit(solution)/shard_map/reduce_scatter | solution.py:254
  756.8 10.8 fusion.55
  810.3 11.0 multiply_reduce_fusion.2
  837.2 22.8 %collective-permute-done.86 = bf16[2,32,4224]{2,1,0:T(8,128)(2,1)S(1)} collective-permute-done((bf16[2,32,4224]{2,1,0:T(8,128)(2,1)S(1)}, bf16[2,32,4224]{2,1,0:T(8,128)(2,1)S(1)}, u32[]{:S(2)}, u32[]{:S(2)}) %collective-permute-start.86) | collective-permute-done | bytes 540704 | tf_op jit(solution)/shard_map/ppermute | solution.py:104
  887.7 27.6 %collective-permute-done.95 = bf16[2,32,2688]{2,1,0:T(8,128)(2,1)S(1)} collective-permute-done((bf16[2,32,2688]{2,1,0:T(8,128)(2,1)S(1)}, bf16[2,32,2688]{2,1,0:T(8,128)(2,1)S(1)}, u32[]{:S(2)}, u32[]{:S(2)}) %collective-permute-start.95) | collective-permute-done | bytes 344096 | tf_op jit(solution)/shard_map/ppermute | solution.py:104
  917.9 17.3 %multiply_reduce_fusion = (f32[16,512]{1,0:T(8,128)S(1)}, f32[16,512,640]{2,1,0:T(8,128)}) fusion(f32[16,512,640]{2,1,0:T(8,128)} %copy-done, f32[16,512]{1,0:T(8,128)S(1)} %copy-done.151, pred[512,640]{1,0:T(8,128)(4,1)S(1)} %copy-done.3, bf16[512,16,64]{0,2,1:T(8,128)(2,1)S(1)} %bitcast.466, bf16[640,16,64]{0,2,1:T(8,128)(2,1)S(1)} %bitcast.461), kind=kOutput, calls=%fused_computation.1 | convolution fusion | flops 697294848 | bytes 44695552 | tf_op jit(solution)/shard_map/qhd,khd->hqk/dot_general | solution.py:360
  942.7 20.1 %multiply_convert_fusion = bf16[16,512,640]{2,1,0:T(8,128)(2,1)} fusion(f32[16,512,640]{2,1,0:T(8,128)} %get-tuple-element.330, f32[16,512,640]{2,1,0:T(8,128)} %copy-done, f32[16,512]{1,0:T(8,128)S(1)} %get-tuple-element.329, f32[16,512]{1,0:T(8,128)S(1)} %copy-done.151, pred[512,640]{1,0:T(8,128)(4,1)S(1)} %copy-done.3), kind=kLoop, calls=%fused_computation | loop fusion | flops 31457280 | bytes 52822016 | tf_op jit(solution)/shard_map/convert_element_type | solution.py:364
  1050.3 22.7 %collective-permute-done.107 = bf16[2,2,32,4224]{3,2,0,1:T(8,128)(2,1)} collective-permute-done((bf16[2,2,32,4224]{3,2,0,1:T(8,128)(2,1)}, bf16[2,2,32,4224]{3,2,0,1:T(8,128)(2,1)}, u32[]{:S(2)}, u32[]{:S(2)}) %collective-permute-start.107) | collective-permute-done | bytes 1081376 | tf_op jit(solution)/shard_map/ppermute | solution.py:104
  1076.7 11.6 collective-permute-done.108
  (1021 shorter events, 773.1 us)
Async XLA Ops:
  14.3 78.1 %all-gather.15.cloned.1.call-start = ((), (), s32[]{:S(2)}) async-start(), calls=%async_computation.15 | async-start | bytes 2580480 | tf_op jit(solution)/shard_map/all_gather | solution.py:184
  23.9 97.5 %all-gather.11.cloned.1.call-start = ((), (), s32[]{:S(2)}) async-start(), calls=%async_computation.13 | async-start | bytes 1351680 | tf_op jit(solution)/shard_map/all_gather | solution.py:184
  26.6 241.1 %all-gather.13.cloned.1.call-start = ((), (), s32[]{:S(2)}) async-start(), calls=%async_computation.14 | async-start | bytes 2580480 | tf_op jit(solution)/shard_map/all_gather | solution.py:184
  95.4 116.7 %collective-permute-start.16 = (bf16[2,32,8064]{2,1,0:T(8,128)(2,1)}, bf16[2,32,8064]{2,1,0:T(8,128)(2,1)}, u32[]{:S(2)}, u32[]{:S(2)}) collective-permute-start(bf16[2,32,8064]{2,1,0:T(8,128)(2,1)} %bitcast.38.refs_1_), channel_id=1, source_target_pairs={{0,8},{4,12},{8,0},{12,4},{16,24},{20,28},{24,16},{28,20},{1,9},{5... | collective-permute-start | bytes 3096584 | tf_op jit(solution)/shard_map/ppermute | solution.py:104
  167.1 507.2 %reduce-scatter.7.cloned.1.call-start = ((), (), s32[]{:S(2)}) async-start(), calls=%async_computation.6 | async-start | bytes 860160 | tf_op jit(solution)/shard_map/reduce_scatter | solution.py:254
  167.3 49.3 %collective-permute-start.17 = (bf16[2,32,8064]{2,1,0:T(8,128)(2,1)}, bf16[2,32,8064]{2,1,0:T(8,128)(2,1)}, u32[]{:S(2)}, u32[]{:S(2)}) collective-permute-start(bf16[2,32,8064]{2,1,0:T(8,128)(2,1)} %bitcast.38.refs_1_), channel_id=1, source_target_pairs={{0,16},{4,20},{8,24},{12,28},{16,0},{20,4},{24,8},{28,12},{1,17},{... | collective-permute-start | bytes 3096584 | tf_op jit(solution)/shard_map/ppermute | solution.py:104
  366.4 45.5 %collective-permute-start.53 = (bf16[2,32,8064]{2,1,0:T(8,128)(2,1)}, bf16[2,32,8064]{2,1,0:T(8,128)(2,1)}, u32[]{:S(2)}, u32[]{:S(2)}) collective-permute-start(bf16[2,32,8064]{2,1,0:T(8,128)(2,1)} %get-tuple-element.265.refs_9_), channel_id=1, source_target_pairs={{0,16},{4,20},{8,24},{12,28},{16,0},{20,4},{24,8},{28,12},{1,17},{... | collective-permute-start | bytes 3096584 | tf_op jit(solution)/shard_map/ppermute | solution.py:104
  368.2 53.8 %collective-permute-start.54 = (bf16[2,32,8064]{2,1,0:T(8,128)(2,1)}, bf16[2,32,8064]{2,1,0:T(8,128)(2,1)}, u32[]{:S(2)}, u32[]{:S(2)}) collective-permute-start(bf16[2,32,8064]{2,1,0:T(8,128)(2,1)} %get-tuple-element.265.refs_9_), channel_id=1, source_target_pairs={{0,8},{4,12},{8,0},{12,4},{16,24},{20,28},{24,16},{28,20},{1,9},{5... | collective-permute-start | bytes 3096584 | tf_op jit(solution)/shard_map/ppermute | solution.py:104
  391.4 42.5 %collective-permute-start.48 = (bf16[2,32,8064]{2,1,0:T(8,128)(2,1)}, bf16[2,32,8064]{2,1,0:T(8,128)(2,1)S(1)}, u32[]{:S(2)}, u32[]{:S(2)}) collective-permute-start(bf16[2,32,8064]{2,1,0:T(8,128)(2,1)} %collective-permute-done.46.refs_2_), channel_id=1, source_target_pairs={{0,16},{4,20},{8,24},{12,28},{16,0},{20,4},{24,8},{28,12},{1,17},{... | collective-permute-start | bytes 3096584 | tf_op jit(solution)/shard_map/ppermute | solution.py:104
  391.5 42.6 %collective-permute-start.50 = (bf16[2,32,8064]{2,1,0:T(8,128)(2,1)}, bf16[2,32,8064]{2,1,0:T(8,128)(2,1)S(1)}, u32[]{:S(2)}, u32[]{:S(2)}) collective-permute-start(bf16[2,32,8064]{2,1,0:T(8,128)(2,1)} %collective-permute-done.46.refs_2_), channel_id=1, source_target_pairs={{0,4},{4,0},{8,12},{12,8},{16,20},{20,16},{24,28},{28,24},{1,5},{5... | collective-permute-start | bytes 3096584 | tf_op jit(solution)/shard_map/ppermute | solution.py:104
  547.8 38.6 %collective-permute-start.66 = (bf16[2,2,32,5376]{3,2,0,1:T(8,128)(2,1)S(1)}, bf16[2,2,32,5376]{3,2,0,1:T(8,128)(2,1)S(1)}, u32[]{:S(2)}, u32[]{:S(2)}) collective-permute-start(bf16[2,2,32,5376]{3,2,0,1:T(8,128)(2,1)S(1)} %bitcast.485), channel_id=1, source_target_pairs={{0,8},{4,12},{8,0},{12,4},{16,24},{20,28},{24,16},{28,20},{1,9},{5... | collective-permute-start | bytes 4128776 | tf_op jit(solution)/shard_map/ppermute | solution.py:104
  652.2 86.3 %reduce-scatter.9.cloned.1.call-start = ((), (), s32[]{:S(2)}) async-start(), calls=%async_computation.7 | async-start | bytes 1720320 | tf_op jit(solution)/shard_map/reduce_scatter | solution.py:254
  695.5 43.0 %collective-permute-start.73 = (bf16[4,2,2,32,4224]{4,3,2,1,0:T(8,128)(2,1)}, bf16[4,2,2,32,4224]{4,3,2,1,0:T(8,128)(2,1)}, u32[]{:S(2)}, u32[]{:S(2)}) collective-permute-start(bf16[4,2,2,32,4224]{4,3,2,1,0:T(8,128)(2,1)} %pad_maximum_fusion.2), channel_id=1, source_target_pairs={{0,4},{4,0},{8,12},{12,8},{16,20},{20,16},{24,28},{28,24},{1,5},{5... | collective-permute-start | bytes 12976136 | tf_op jit(solution)/shard_map/ppermute | solution.py:104
  702.6 285.1 %reduce-scatter.11.cloned.1.call-start = ((), (), s32[]{:S(2)}) async-start(), calls=%async_computation.8 | async-start | bytes 1351680 | tf_op jit(solution)/shard_map/reduce_scatter | solution.py:254
  706.8 61.4 %collective-permute-start.74 = (bf16[1,32,2688]{2,1,0:T(8,128)(2,1)}, bf16[1,32,2688]{2,1,0:T(8,128)(2,1)}, u32[]{:S(2)}, u32[]{:S(2)}) collective-permute-start(bf16[1,32,2688]{2,1,0:T(8,128)(2,1)} %bitcast.95.refs_1_), channel_id=1, source_target_pairs={{0,16},{4,20},{8,24},{12,28},{16,0},{20,4},{24,8},{28,12},{1,17},{... | collective-permute-start | bytes 516104 | tf_op jit(solution)/shard_map/ppermute | solution.py:104
  744.4 41.7 %collective-permute-start.77 = (bf16[2,2,32,4224]{3,2,0,1:T(8,128)(2,1)}, bf16[2,2,32,4224]{3,2,0,1:T(8,128)(2,1)S(1)}, u32[]{:S(2)}, u32[]{:S(2)}) collective-permute-start(bf16[2,2,32,4224]{3,2,0,1:T(8,128)(2,1)} %bitcast.402), channel_id=1, source_target_pairs={{0,8},{4,12},{8,0},{12,4},{16,24},{20,28},{24,16},{28,20},{1,9},{5... | collective-permute-start | bytes 3244040 | tf_op jit(solution)/shard_map/ppermute | solution.py:104
  806.6 54.0 %collective-permute-start.90 = (bf16[4,2,2,32,5376]{4,3,2,1,0:T(8,128)(2,1)}, bf16[4,2,2,32,5376]{4,3,2,1,0:T(8,128)(2,1)S(1)}, u32[]{:S(2)}, u32[]{:S(2)}) collective-permute-start(bf16[4,2,2,32,5376]{4,3,2,1,0:T(8,128)(2,1)} %dynamic-slice_bitcast_fusion), channel_id=1, source_target_pairs={{0,4},{4,0},{8,12},{12,8},{16,20},{20,16},{24,28},{28,24},{1,5},{5... | collective-permute-start | bytes 16515080 | tf_op jit(solution)/shard_map/ppermute | solution.py:104
  872.4 42.8 %collective-permute-start.97 = (bf16[2,2,32,5376]{3,2,0,1:T(8,128)(2,1)}, bf16[2,2,32,5376]{3,2,0,1:T(8,128)(2,1)}, u32[]{:S(2)}, u32[]{:S(2)}) collective-permute-start(bf16[2,2,32,5376]{3,2,0,1:T(8,128)(2,1)} %bitcast.396), channel_id=1, source_target_pairs={{0,8},{4,12},{8,0},{12,4},{16,24},{20,28},{24,16},{28,20},{1,9},{5... | collective-permute-start | bytes 4128776 | tf_op jit(solution)/shard_map/ppermute | solution.py:104
  875.8 40.2 %collective-permute-start.98 = (bf16[2,2,32,5376]{3,2,0,1:T(8,128)(2,1)}, bf16[2,2,32,5376]{3,2,0,1:T(8,128)(2,1)}, u32[]{:S(2)}, u32[]{:S(2)}) collective-permute-start(bf16[2,2,32,5376]{3,2,0,1:T(8,128)(2,1)} %bitcast.395), channel_id=1, source_target_pairs={{0,16},{4,20},{8,24},{12,28},{16,0},{20,4},{24,8},{28,12},{1,17},{... | collective-permute-start | bytes 4128776 | tf_op jit(solution)/shard_map/ppermute | solution.py:104
  878.0 130.5 %reduce-scatter.13.cloned.1.call-start = ((), (), s32[]{:S(2)}) async-start(), calls=%async_computation.9 | async-start | bytes 860160 | tf_op jit(solution)/shard_map/reduce_scatter | solution.py:254
  937.8 49.8 %collective-permute-start.99 = (bf16[2,32,5376]{2,1,0:T(8,128)(2,1)}, bf16[2,32,5376]{2,1,0:T(8,128)(2,1)}, u32[]{:S(2)}, u32[]{:S(2)}) collective-permute-start(bf16[2,32,5376]{2,1,0:T(8,128)(2,1)} %dynamic-slice_bitcast_fusion.13), channel_id=1, source_target_pairs={{0,16},{4,20},{8,24},{12,28},{16,0},{20,4},{24,8},{28,12},{1,17},{... | collective-permute-start | bytes 2064392 | tf_op jit(solution)/shard_map/ppermute | solution.py:104
  941.4 46.3 %collective-permute-start.100 = (bf16[2,32,5376]{2,1,0:T(8,128)(2,1)}, bf16[2,32,5376]{2,1,0:T(8,128)(2,1)}, u32[]{:S(2)}, u32[]{:S(2)}) collective-permute-start(bf16[2,32,5376]{2,1,0:T(8,128)(2,1)} %dynamic-slice_bitcast_fusion.12), channel_id=1, source_target_pairs={{0,8},{4,12},{8,0},{12,4},{16,24},{20,28},{24,16},{28,20},{1,9},{5... | collective-permute-start | bytes 2064392 | tf_op jit(solution)/shard_map/ppermute | solution.py:104
  977.8 123.4 %reduce-scatter.17.cloned.1.call-start = ((), (), s32[]{:S(2)}) async-start(), calls=%async_computation.11 | async-start | bytes 1720320 | tf_op jit(solution)/shard_map/reduce_scatter | solution.py:254
  1049.8 90.1 %reduce-scatter.15.cloned.1.call-start = ((), (), s32[]{:S(2)}) async-start(), calls=%async_computation.10 | async-start | bytes 1351680 | tf_op jit(solution)/shard_map/reduce_scatter | solution.py:254
  (340 other events, 4889.1 us)
Sparse Core Ops, SparseCore 0:
  14.5 31.2 all-gather.8
  47.9 44.4 all-gather.14
  94.0 27.3 all-gather.10
  167.2 43.5 all-gather.12
  652.3 21.9 reduce-scatter.6
  702.7 35.7 reduce-scatter.8
  878.1 25.8 reduce-scatter.10
  977.9 20.6 reduce-scatter.12
  1049.9 29.2 reduce-scatter.16
  1090.7 26.0 reduce-scatter.14
